TPU v7x, 32 devices: a whole 2x2x4 slice. The times are simulated.
32 devices in a mesh: dp: 16 (over z, y, x), seq: 2 (over core).
Axes of the slice: x: 2, y: 2, z: 4, core: 2. Of those that a mesh axis runs over, the one named last changes fastest.
Arguments:
- tokens: bfloat16 [16, 2048, 1120], P('dp', 'seq'), may hold values from -6 to 6
- cotangent: bfloat16 [16, 2048, 1120], P('dp', 'seq'), may hold values from -6 to 6
- pad_mask: int32 [16, 2048], P('dp', 'seq'), may hold values from 0 to 1, as said below
- prefix_len: int32 [16], P('dp'), may hold values from 1 to 128
- norm_gains: float32 [2, 1120], replicated, may hold values from 0.5 to 1.5
- norm_shifts: float32 [2, 1120], replicated, may hold values from -1.8 to 1.8
- owner_map: int32 [192], replicated, may hold values from 0 to 191, as said below
- weight_copy: bfloat16 [192, 280, 280], P('dp'), may hold values from -1.8090681 to 1.8090681
- master: float32 [192, 280, 280], P('dp'), may hold values from -1.8090681 to 1.8090681
- average_weights: float32 [192, 280, 280], P('dp'), may hold values from -1.8090681 to 1.8090681
- stat_left: float32 [192, 280, 280], P('dp'), may hold values from -16.290909 to 36.654545, as said below
- stat_right: float32 [192, 280, 280], P('dp'), may hold values from -16.290909 to 36.654545, as said below
- root_left: float32 [192, 280, 280], P('dp'), may hold values from -3 to 5, as said below
- root_right: float32 [192, 280, 280], P('dp'), may hold values from -3 to 5, as said below
Outputs:
- block_out: bfloat16 [16, 2048, 1120], P('dp', 'seq')
- grad_input: float32 [16, 2048, 1120], P('dp', 'seq')
- norm_grad: float32 [4, 1120], replicated
- new_norms: float32 [4, 1120], replicated
- slot_grad: float32 [192, 280, 280], P('dp')
- new_left: float32 [192, 280, 280], P('dp')
- new_right: float32 [192, 280, 280], P('dp')
- new_master: float32 [192, 280, 280], P('dp')
- new_copy: bfloat16 [192, 280, 280], P('dp')
- new_average: float32 [192, 280, 280], P('dp')
Inputs may be any that keep to these rules, and one draw needn't show every extreme that they name: `pad_mask`: in each cell the ones come first, 512 or more of them; some cell has no zeros. `owner_map`: each block number appears once. `stat_left`: Symmetric. `stat_right`: Symmetric. `root_left`: Symmetric. `root_right`: Symmetric.
All inputs are finite; a program needn't handle non-finite values.
Results may differ from a plain program's by a relative error of at most 0.0085.
Values may be sent and summed in bfloat16 or wider, within the bound.
A program may use at most 448 MiB of HBM per device.

v0:
```python
import math
import jax
import jax.numpy as jnp
from jax import lax
from jax.sharding import PartitionSpec as P

HEADS = 20
GB = 256
PREFIX = 128
highest = lax.Precision.HIGHEST


def spread(block, axis, holder):
    block = jnp.where(lax.axis_index(axis) == holder, block, jnp.zeros_like(block))
    return lax.psum(block, axis)


def layer_norm(values, gain_row, shift_row):
    average = jnp.mean(values, axis=-1, keepdims=True)
    centred = values - average
    variance = jnp.mean(centred * centred, axis=-1, keepdims=True)
    return centred * lax.rsqrt(variance + 1e-05) * gain_row + shift_row


def gelu_tanh(values):
    return jax.nn.gelu(values, approximate=True)


def assemble(pieces, row_blocks, col_blocks):
    block_size = pieces.shape[-1]
    return (
        pieces.reshape(row_blocks, col_blocks, block_size, block_size)
        .transpose(0, 2, 1, 3)
        .reshape(row_blocks * block_size, col_blocks * block_size)
    )


def split_blocks(matrix, block_size):
    row_count, col_count = matrix.shape
    return (
        matrix.reshape(row_count // block_size, block_size, col_count // block_size, block_size)
        .transpose(0, 2, 1, 3)
        .reshape(-1, block_size, block_size)
    )


def matmul(left, right):
    return jnp.dot(left, right, preferred_element_type=jnp.float32)


def local(
    tokens,
    cotangent,
    pad_mask,
    prefix_len,
    norm_gains,
    norm_shifts,
    owner_map,
    weight_copy,
    master,
    average_weights,
    stat_left,
    stat_right,
    root_left,
    root_right,
):
    cell_count, group_len, features = tokens.shape
    row_count = cell_count * group_len
    head_size = features // HEADS
    per_group = group_len // GB
    score_scale = head_size ** (-0.5)
    slots = lax.all_gather(weight_copy, "dp", axis=0, tiled=True)
    block_count = slots.shape[0]
    block_size = slots.shape[-1]
    row_blocks = features // block_size
    col_blocks = (block_count - 4 * row_blocks * row_blocks) // (2 * row_blocks)
    square = row_blocks * row_blocks
    inverse = (
        jnp.zeros((block_count,), jnp.int32)
        .at[owner_map]
        .set(jnp.arange(block_count, dtype=jnp.int32))
    )
    blocks = jnp.take(slots, inverse, axis=0)
    w_query = assemble(blocks[0:square], row_blocks, row_blocks)
    w_key = assemble(blocks[square : 2 * square], row_blocks, row_blocks)
    w_value = assemble(blocks[2 * square : 3 * square], row_blocks, row_blocks)
    w_out = assemble(blocks[3 * square : 4 * square], row_blocks, row_blocks)
    w_up = assemble(
        blocks[4 * square : 4 * square + row_blocks * col_blocks], row_blocks, col_blocks
    )
    w_down = assemble(blocks[4 * square + row_blocks * col_blocks :], col_blocks, row_blocks)
    inputs = tokens.astype(jnp.float32).reshape(row_count, features)
    normed_one, norm_one_back = jax.vjp(layer_norm, inputs, norm_gains[0], norm_shifts[0])
    normed_in = normed_one.astype(jnp.bfloat16)
    queries = matmul(normed_in, w_query).astype(jnp.bfloat16)
    key_rows = matmul(normed_in, w_key).astype(jnp.bfloat16)
    value_rows = matmul(normed_in, w_value).astype(jnp.bfloat16)
    block_shape = (cell_count, per_group, GB, HEADS, head_size)
    query_blocks = queries.reshape(block_shape)
    key_blocks = key_rows.reshape(block_shape)
    value_blocks = value_rows.reshape(block_shape)
    key_cells = key_rows.reshape(cell_count, group_len, HEADS, head_size)
    value_cells = value_rows.reshape(cell_count, group_len, HEADS, head_size)
    prefix_keys, prefix_values = (
        spread(key_cells[:, :PREFIX], "seq", 0),
        spread(value_cells[:, :PREFIX], "seq", 0),
    )
    seq_index = lax.axis_index("seq")
    position = seq_index * group_len + jnp.arange(group_len, dtype=jnp.int32)
    alive_keys = jnp.where(
        position[None, :] < PREFIX, position[None, :] < prefix_len[:, None], pad_mask == 1
    )
    prefix_alive = jnp.arange(PREFIX, dtype=jnp.int32)[None, :] < prefix_len[:, None]
    offsets = jnp.arange(GB)
    local_seen = alive_keys.reshape(cell_count, per_group, 1, 1, GB) & (
        offsets[:, None] >= offsets[None, :]
    )
    later_block = seq_index * per_group + jnp.arange(per_group) > 0
    prefix_seen = prefix_alive[:, None, None, None, :] & later_block[None, :, None, None, None]
    visible = jnp.concatenate(
        [jnp.broadcast_to(prefix_seen, (cell_count, per_group, 1, GB, PREFIX)), local_seen], axis=-1
    )

    def score_rows():
        raw_prefix = jnp.einsum(
            "cnqhd,ckhd->cnhqk", query_blocks, prefix_keys, preferred_element_type=jnp.float32
        )
        raw_local = jnp.einsum(
            "cnqhd,cnkhd->cnhqk", query_blocks, key_blocks, preferred_element_type=jnp.float32
        )
        return jnp.where(
            visible, jnp.concatenate([raw_prefix, raw_local], axis=-1) * score_scale, -1e30
        )

    scores = score_rows()
    row_max = jnp.max(scores, axis=-1, keepdims=True)
    log_total = row_max + jnp.log(jnp.sum(jnp.exp(scores - row_max), axis=-1, keepdims=True))
    weights_low = jnp.exp(scores - log_total).astype(jnp.bfloat16)
    attended = jnp.einsum(
        "cnhqk,ckhd->cnqhd",
        weights_low[..., :PREFIX],
        prefix_values,
        preferred_element_type=jnp.float32,
    )
    attended = attended + jnp.einsum(
        "cnhqk,cnkhd->cnqhd",
        weights_low[..., PREFIX:],
        value_blocks,
        preferred_element_type=jnp.float32,
    )
    attended_low = attended.reshape(row_count, features).astype(jnp.bfloat16)
    middle = inputs + matmul(attended_low, w_out)
    normed_two, norm_two_back = jax.vjp(layer_norm, middle, norm_gains[1], norm_shifts[1])
    normed_mid = normed_two.astype(jnp.bfloat16)
    up_pre = matmul(normed_mid, w_up)
    activated, gelu_back = jax.vjp(gelu_tanh, up_pre)
    activated_low = activated.astype(jnp.bfloat16)
    block_out = (
        (middle + matmul(activated_low, w_down))
        .astype(jnp.bfloat16)
        .reshape(cell_count, group_len, features)
    )
    grad_rows = cotangent.astype(jnp.float32).reshape(row_count, features)
    grad_low = cotangent.reshape(row_count, features)
    grad_down = matmul(activated_low.T, grad_low)
    grad_act = matmul(grad_low, w_down.T)
    grad_pre = gelu_back(grad_act)[0].astype(jnp.bfloat16)
    grad_up = matmul(normed_mid.T, grad_pre)
    grad_mid_in = matmul(grad_pre, w_up.T)
    grad_middle_n, grad_gain_two, grad_shift_two = norm_two_back(grad_mid_in)
    grad_middle = grad_rows + grad_middle_n
    grad_branch = grad_middle.astype(jnp.bfloat16)
    grad_out = matmul(attended_low.T, grad_branch)
    grad_att = matmul(grad_branch, w_out.T).astype(jnp.bfloat16).reshape(block_shape)
    key_weights = jnp.exp(score_rows() - log_total)
    weights_again = key_weights.astype(jnp.bfloat16)
    grad_prob = jnp.concatenate(
        [
            jnp.einsum(
                "cnqhd,ckhd->cnhqk", grad_att, prefix_values, preferred_element_type=jnp.float32
            ),
            jnp.einsum(
                "cnqhd,cnkhd->cnhqk", grad_att, value_blocks, preferred_element_type=jnp.float32
            ),
        ],
        axis=-1,
    )
    grad_score = key_weights * (
        grad_prob - jnp.sum(key_weights * grad_prob, axis=-1, keepdims=True)
    )
    grad_raw = (grad_score * score_scale).astype(jnp.bfloat16)
    grad_raw_prefix = grad_raw[..., :PREFIX]
    grad_raw_local = grad_raw[..., PREFIX:]
    grad_query = jnp.einsum(
        "cnhqk,ckhd->cnqhd", grad_raw_prefix, prefix_keys, preferred_element_type=jnp.float32
    )
    grad_query = grad_query + jnp.einsum(
        "cnhqk,cnkhd->cnqhd", grad_raw_local, key_blocks, preferred_element_type=jnp.float32
    )
    grad_key = jnp.einsum(
        "cnhqk,cnqhd->cnkhd", grad_raw_local, query_blocks, preferred_element_type=jnp.float32
    )
    grad_value = jnp.einsum(
        "cnhqk,cnqhd->cnkhd",
        weights_again[..., PREFIX:],
        grad_att,
        preferred_element_type=jnp.float32,
    )
    grad_key_pre = jnp.einsum(
        "cnhqk,cnqhd->ckhd", grad_raw_prefix, query_blocks, preferred_element_type=jnp.float32
    )
    grad_value_pre = jnp.einsum(
        "cnhqk,cnqhd->ckhd",
        weights_again[..., :PREFIX],
        grad_att,
        preferred_element_type=jnp.float32,
    )
    summed_key, summed_value = lax.psum((grad_key_pre, grad_value_pre), "seq")
    is_owner = (seq_index == 0).astype(jnp.float32)
    grad_key = (
        grad_key.reshape(cell_count, group_len, features)
        .at[:, :PREFIX]
        .add(is_owner * summed_key.reshape(cell_count, PREFIX, features))
    )
    grad_value = (
        grad_value.reshape(cell_count, group_len, features)
        .at[:, :PREFIX]
        .add(is_owner * summed_value.reshape(cell_count, PREFIX, features))
    )
    query_grad_low = grad_query.reshape(row_count, features).astype(jnp.bfloat16)
    key_grad_low = grad_key.reshape(row_count, features).astype(jnp.bfloat16)
    value_grad_low = grad_value.reshape(row_count, features).astype(jnp.bfloat16)
    grad_wq = matmul(normed_in.T, query_grad_low)
    grad_wk = matmul(normed_in.T, key_grad_low)
    grad_wv = matmul(normed_in.T, value_grad_low)
    grad_normed = (
        matmul(query_grad_low, w_query.T)
        + matmul(key_grad_low, w_key.T)
        + matmul(value_grad_low, w_value.T)
    )
    grad_in_n, grad_gain_one, grad_shift_one = norm_one_back(grad_normed)
    grad_input = (grad_middle + grad_in_n).reshape(cell_count, group_len, features)
    grad_scale = 1.0 / math.sqrt(row_count * lax.axis_size("dp") * lax.axis_size("seq"))
    norm_terms = (
        jnp.stack([grad_gain_one, grad_shift_one, grad_gain_two, grad_shift_two]) * grad_scale
    )
    norm_grad = lax.psum(norm_terms, ("dp", "seq"))
    params = jnp.stack([norm_gains[0], norm_shifts[0], norm_gains[1], norm_shifts[1]])
    new_norms = params - 0.1 * norm_grad * lax.rsqrt(jnp.mean(norm_grad * norm_grad) + 1e-06)
    grad_blocks = (
        jnp.concatenate(
            [
                split_blocks(matrix, block_size)
                for matrix in (grad_wq, grad_wk, grad_wv, grad_out, grad_up, grad_down)
            ],
            axis=0,
        )
        * grad_scale
    )
    ordered = jnp.take(grad_blocks, owner_map, axis=0)
    owned_part = lax.psum_scatter(ordered, "dp", scatter_dimension=0, tiled=True)
    slot_grad = lax.psum(owned_part, "seq")
    new_left = (
        0.5 * stat_left
        + 0.5 * jnp.einsum("sij,skj->sik", slot_grad, slot_grad, precision=highest) / block_size
    )
    new_right = (
        0.5 * stat_right
        + 0.5 * jnp.einsum("sji,sjk->sik", slot_grad, slot_grad, precision=highest) / block_size
    )
    right_part = jnp.einsum("sij,sjk->sik", slot_grad, root_right, precision=highest)
    precond = jnp.einsum("sij,sjk->sik", root_left, right_part, precision=highest)
    new_master = master - 0.03 * precond
    new_copy = new_master.astype(jnp.bfloat16)
    new_average = 0.8 * average_weights + 0.2 * new_master
    return (
        block_out,
        grad_input,
        norm_grad,
        new_norms,
        slot_grad,
        new_left,
        new_right,
        new_master,
        new_copy,
        new_average,
    )


def solution(mesh):
    in_specs = (
        P("dp", "seq", None),
        P("dp", "seq", None),
        P("dp", "seq"),
        P("dp"),
        P(),
        P(),
        P(),
        P("dp", None, None),
        P("dp", None, None),
        P("dp", None, None),
        P("dp", None, None),
        P("dp", None, None),
        P("dp", None, None),
        P("dp", None, None),
    )
    out_specs = (
        P("dp", "seq", None),
        P("dp", "seq", None),
        P(),
        P(),
        P("dp", None, None),
        P("dp", None, None),
        P("dp", None, None),
        P("dp", None, None),
        P("dp", None, None),
        P("dp", None, None),
    )
    return jax.shard_map(local, mesh=mesh, in_specs=in_specs, out_specs=out_specs, check_vma=False)
```

profile of v0, /device:TPU:0, one launch (start us, length us, event | category | flops | bytes accessed | tf_op | source)
XLA Modules:
  0.0 2638.7 jit_solution(1818044440257464110)
XLA Ops:
  16.7 420.8 %all-gather.2.cloned.1.call-done = bf16[192,280,280]{2,1,0:T(8,128)(2,1)} async-done(((bf16[12,280,280]{2,1,0:T(8,128)(2,1)}), bf16[192,280,280]{2,1,0:T(8,128)(2,1)}) %all-gather.2.cloned.1.call-update) | async-done | bytes 30105616 | tf_op jit(solution)/shard_map/all_gather | solution.py:72
  437.5 28.3 %gather_fusion = bf16[192,280,280]{2,1,0:T(8,128)(2,1)} fusion(bf16[192,280,280]{2,1,0:T(8,128)(2,1)} %all-gather.2.cloned.1.call-done, s32[1024]{0:T(1024)S(1)} %pad_clamp_fusion.1), kind=kCustom, calls=%fused_computation | custom fusion | bytes 60211968 | tf_op jit(solution)/shard_map/jit(_take)/gather | solution.py:83
  465.8 28.1 %broadcast_select_fusion.1 = bf16[192,280,280]{2,1,0:T(8,128)(2,1)} fusion(bf16[192,280,280]{2,1,0:T(8,128)(2,1)} %gather_fusion, pred[192]{0:T(512)(128)(4,1)S(1)} %compare_and_fusion.1), kind=kLoop, calls=%fused_computation.5 | loop fusion | flops 15052800 | bytes 60211392 | tf_op jit(solution)/shard_map/jit(_take)/select_n | solution.py:83
  503.2 21.0 fusion.110
  601.5 22.4 copy.115
  623.9 21.1 reshape.779
  659.3 21.4 reshape.777
  741.5 26.2 fusion.16
  767.8 31.0 %fusion.8 = bf16[1024,4480]{1,0:T(8,128)(2,1)} fusion(f32[1024,4480]{1,0:T(8,128)} %get-tuple-element.100, bf16[4480,1120]{0,1:T(8,128)(2,1)} %reshape.779, bf16[1,1024,1120]{1,2,0:T(8,128)(2,1)S(1)} %copy-done.12), kind=kOutput, calls=%fused_computation.23 | convolution fusion | flops 10367795200 | bytes 39854080 | tf_op jit(solution)/shard_map/dot_general | solution.py:48
  798.8 19.8 multiply_reduce_fusion.1
  861.1 20.7 multiply_reduce_fusion
  881.8 22.1 multiply_convert_fusion
  930.5 18.1 fusion.103
  988.5 28.5 %reshape.801 = f32[4,280,16,280]{3,2,1,0:T(8,128)} reshape(f32[1120,4480]{1,0:T(8,128)} %fusion.103) | data formatting | bytes 40140800 | tf_op jit(solution)/shard_map/reshape | solution.py:41
  1017.1 27.0 %copy.138 = f32[4,280,16,280]{3,1,2,0:T(8,128)} copy(f32[4,280,16,280]{3,2,1,0:T(8,128)} %reshape.801) | data formatting | bytes 40140800 | tf_op jit(solution)/shard_map/reshape | solution.py:41
  1056.8 20.0 fusion.117
  1155.3 20.5 constant_dynamic-update-slice_fusion
  1175.8 55.9 %broadcast_multiply_fusion = f32[192,280,280]{2,1,0:T(8,128)} fusion(f32[192,280,280]{2,1,0:T(8,128)} %constant_dynamic-update-slice_fusion), kind=kLoop, calls=%fused_computation.4 | loop fusion | flops 15052800 | bytes 120422400 | tf_op jit(solution)/shard_map/mul | solution.py:251
  1231.7 56.4 %gather_fusion.1 = f32[192,280,280]{2,1,0:T(8,128)} fusion(f32[192,280,280]{2,1,0:T(8,128)} %broadcast_multiply_fusion, s32[1024]{0:T(1024)} %pad_clamp_fusion), kind=kCustom, calls=%fused_computation.1 | custom fusion | bytes 120423168 | tf_op jit(solution)/shard_map/jit(_take)/gather | solution.py:260
  1288.1 54.1 %broadcast_select_fusion = f32[192,280,280]{2,1,0:T(8,128)} fusion(f32[192,280,280]{2,1,0:T(8,128)} %gather_fusion.1, pred[192]{0:T(512)(128)(4,1)S(1)} %copy-done.57), kind=kLoop, calls=%fused_computation.3 | loop fusion | flops 15052800 | bytes 120422592 | tf_op jit(solution)/shard_map/jit(_take)/select_n | solution.py:260
  1342.2 1134.6 %reduce-scatter.2.cloned.1.call-done = f32[12,280,280]{2,1,0:T(8,128)} async-done(((f32[192,280,280]{2,1,0:T(8,128)}), f32[12,280,280]{2,1,0:T(8,128)}) %reduce-scatter.2.cloned.1.call-update) | async-done | bytes 3763216 | tf_op jit(solution)/shard_map/reduce_scatter | solution.py:261
  2489.6 19.8 fusion.54
  2509.4 39.9 %psum.46 = f32[4,1120]{1,0:T(4,128)S(1)} all-reduce(f32[4,1120]{1,0:T(4,128)S(1)} %maximum_multiply_fusion.1), channel_id=1, replica_groups=mesh['dp'=16,'seq'=2] {'dp','seq'}, use_global_device_ids=true, to_apply=%region_20.21 | all-reduce | flops 4480 | bytes 35840 | tf_op jit(solution)/shard_map/psum | solution.py:247
  2565.4 17.3 multiply_add_fusion
  (298 shorter events, 447.2 us)
Async XLA Ops:
  7.2 430.3 %all-gather.2.cloned.1.call-start = ((), (), s32[]{:S(2)}) async-start(), calls=%async_computation.1 | async-start | bytes 43868160 | tf_op jit(solution)/shard_map/all_gather | solution.py:72
  7.9 684.3 %all-reduce.10.cloned.1.call-start = ((), (), s32[]{:S(2)}) async-start(), calls=%async_computation.5 | async-start | bytes 1146880 | tf_op jit(solution)/shard_map/psum | solution.py:15
  14.2 555.5 %copy-start.34 = (f32[1024]{0:T(1024)}, f32[1024]{0:T(1024)S(1)}, u32[]{:S(2)}) copy-start(f32[1024]{0:T(1024)S(1)} %broadcast_multiply_fusion.4) | copy-start | bytes 12292
  15.5 554.3 %copy-start.40 = (f32[1024]{0:T(1024)}, f32[1024]{0:T(1024)S(1)}, u32[]{:S(2)}) copy-start(f32[1024]{0:T(1024)S(1)} %fusion.95) | copy-start | bytes 12292
  16.7 553.0 %copy-start.32 = (f32[1120]{0:T(1024)}, f32[1120]{0:T(1024)S(1)}, u32[]{:S(2)}) copy-start(f32[1120]{0:T(1024)S(1)} %get-tuple-element.104) | copy-start | bytes 13444
  16.7 553.0 %copy-start.42 = (f32[1120]{0:T(1024)}, f32[1120]{0:T(1024)S(1)}, u32[]{:S(2)}) copy-start(f32[1120]{0:T(1024)S(1)} %get-tuple-element.73) | copy-start | bytes 13444
  569.7 517.7 %all-reduce.8.cloned.1.call-start = ((), (), s32[]{:S(2)}) async-start(), calls=%async_computation.4 | async-start | bytes 2293760 | tf_op jit(solution)/shard_map/psum | solution.py:218
  589.3 103.0 %copy-start.2 = (bf16[4,256,20,56]{1,0,3,2:T(4,128)(2,1)}, bf16[4,256,20,56]{1,0,3,2:T(4,128)(2,1)S(1)}, u32[]{:S(2)}) copy-start(bf16[4,256,20,56]{1,0,3,2:T(4,128)(2,1)S(1)} %reshape.769) | copy-start | bytes 6881284
  695.0 21.3 copy-start
  740.9 77.7 %copy-start.8 = (f32[1024,1120]{0,1:T(8,128)}, f32[1024,1120]{0,1:T(8,128)S(1)}, u32[]{:S(2)}) copy-start(f32[1024,1120]{0,1:T(8,128)S(1)} %get-tuple-element.95) | copy-start | bytes 13762564
  741.5 26.3 copy-start.12
  881.8 27.6 %copy-start.3 = (bf16[4,256,20,56]{1,0,3,2:T(4,128)(2,1)S(1)}, bf16[4,256,20,56]{1,0,3,2:T(4,128)(2,1)}, u32[]{:S(2)}) copy-start(bf16[4,256,20,56]{1,0,3,2:T(4,128)(2,1)} %copy-done.2) | copy-start | bytes 6881284
  920.8 27.8 %slice-start.18 = ((s8[4587520]{0:T(1024)(128)(4,1)}), s8[4194304]{0:T(1024)(128)(4,1)S(1)}, s32[]{:S(2)}) async-start(s8[4587520]{0:T(1024)(128)(4,1)} %bitcast.354), calls=%async_computation.24 | async-start | bytes 8388608
  1056.7 1420.1 %reduce-scatter.2.cloned.1.call-start = ((), (), s32[]{:S(2)}) async-start(), calls=%async_computation.2 | async-start | bytes 87736320 | tf_op jit(solution)/shard_map/reduce_scatter | solution.py:261
  1121.3 24.5 slice-start.7
  1121.3 24.5 slice-start.8
  1121.3 24.5 slice-start.9
  1231.7 56.4 %copy-start.57 = (pred[192]{0:T(512)(128)(4,1)S(1)}, pred[192]{0:T(512)(128)(4,1)}, u32[]{:S(2)}) copy-start(pred[192]{0:T(512)(128)(4,1)} %compare_and_fusion) | copy-start | bytes 580
  1342.2 1209.1 %all-reduce.6.cloned.1.call-start = ((), (), s32[]{:S(2)}) async-start(), calls=%async_computation.3 | async-start | bytes 10321920 | tf_op jit(solution)/shard_map/psum | solution.py:262
  2489.5 61.1 %copy-start.47 = (f32[1,1120]{1,0:T(1,128)S(1)}, f32[1,1120]{1,0:T(1,128)}, u32[]{:S(2)}) copy-start(f32[1,1120]{1,0:T(1,128)} %get-tuple-element.91) | copy-start | bytes 13444
  2489.5 61.1 %copy-start.48 = (f32[1,1120]{1,0:T(1,128)S(1)}, f32[1,1120]{1,0:T(1,128)}, u32[]{:S(2)}) copy-start(f32[1,1120]{1,0:T(1,128)} %get-tuple-element.93) | copy-start | bytes 13444
  2489.5 61.1 %copy-start.49 = (f32[1,1120]{1,0:T(1,128)S(1)}, f32[1,1120]{1,0:T(1,128)}, u32[]{:S(2)}) copy-start(f32[1,1120]{1,0:T(1,128)} %get-tuple-element.102) | copy-start | bytes 13444
  2489.6 61.1 %copy-start.50 = (f32[1,1120]{1,0:T(1,128)S(1)}, f32[1,1120]{1,0:T(1,128)}, u32[]{:S(2)}) copy-start(f32[1,1120]{1,0:T(1,128)} %get-tuple-element.103) | copy-start | bytes 13444
  2591.6 23.1 slice-start.5
  (63 other events, 547.7 us)
Sparse Core Ops, SparseCore 0:
  10.8 426.5 all-gather.1
  569.8 17.0 all-reduce.9
  1056.8 18.0 all-reduce.7
  1342.3 1134.4 reduce-scatter.1
  2479.3 29.0 all-reduce.5
where the time goes:
time: 2650 us; the launch traced here: 2640 us
  waiting for transfers between devices  1560 us (59%)
  local copies, waits for them, and re-layouts  452 us (17%)
  matrix products  338 us (13%)
  other arithmetic  236 us (9%)
  blocking collectives  39.9 us (2%)
    reduce_scatter x1, waiting for transfers between devices, local(): lax.psum_scatter(ordered, 'dp', scatter_dimension=0, tiled=True)  1130 us
    all_gather x1, waiting for transfers between devices, local(): slots = lax.all_gather(weight_copy, 'dp', axis=0, tiled=True)  421 us
    dot_general x18, matrix products, matmul(): return jnp.dot(left, right, preferred_element_type=jnp.float32)  197 us
    unnamed x179, local copies, waits for them, and re-layouts  81.6 us
    reshape x6, local copies, waits for them, and re-layouts, assemble(): return pieces.reshape(row_blocks, col_blocks, block_size, block_size).tra...  67.7 us
    gather x1, local copies, waits for them, and re-layouts, local(): ordered = jnp.take(grad_blocks, owner_map, axis=0)  56.4 us
    mul x1, other arithmetic, local(): jnp.concatenate([split_blocks(matrix, block_size) for matrix in (grad_wq,...  55.9 us
    reshape x2, local copies, waits for them, and re-layouts, split_blocks(): matrix.reshape(row_count // block_size, block_size, col_count // block_si...  55.5 us
  transfers between devices with their start and end apart: 5, of which 2 were waited for; matrix products, arithmetic and copies ran while one was open for 7% of the time, Pallas kernels for 0%

commit v1 on v0

--- a/solution.py
+++ b/solution.py
@@ -69,7 +69,16 @@
     head_size = features // HEADS
     per_group = group_len // GB
     score_scale = head_size ** (-0.5)
-    slots = lax.all_gather(weight_copy, "dp", axis=0, tiled=True)
+    devs = lax.axis_size("dp")
+    samples = [weight_copy]
+    for at in range(1, devs):
+        samples.append(
+            lax.ppermute(
+                samples[at - 1], axis_name="dp", perm=[(t, (t - 1) % devs) for t in range(devs)]
+            )
+        )
+    y1 = jnp.concatenate(samples, axis=0)
+    slots = jnp.roll(y1, lax.axis_index("dp") * weight_copy.shape[0], axis=0)
     block_count = slots.shape[0]
     block_size = slots.shape[-1]
     row_blocks = features // block_size

time: 2650 us -> 3150 us (1.19)
  waiting for transfers between devices: 1560 us -> 1850 us
  local copies, waits for them, and re-layouts: 452 us -> 563 us
  starting transfers between devices: 0.2 us -> 92.6 us
    ppermute x0 -> x15, waiting for transfers between devices: none -> 714 us  [local(): lax.ppermute(samples[at - 1], axis_name='dp', perm=[(t, (t - 1) % devs) f...]
    all_gather x1 -> x0, waiting for transfers between devices: 421 us -> none  [local(): slots = lax.all_gather(weight_copy, 'dp', axis=0, tiled=True)]
    ppermute x0 -> x15, starting transfers between devices: none -> 92.4 us  [local(): lax.ppermute(samples[at - 1], axis_name='dp', perm=[(t, (t - 1) % devs) f...]
    unnamed x179 -> x254, local copies, waits for them, and re-layouts: 81.6 us -> 163 us
  transfers between devices with their start and end apart: 5 -> 19, of which waited for: 2 -> 16; matrix products, arithmetic and copies ran while one was open for 7% -> 7% of each run, Pallas kernels for 0% -> 0%
where the time goes in v1:
time: 3150 us; the launch traced here: 3140 us
  waiting for transfers between devices  1850 us (59%)
  local copies, waits for them, and re-layouts  563 us (18%)
  matrix products  338 us (11%)
  other arithmetic  237 us (8%)
  starting transfers between devices  92.6 us (3%)
  blocking collectives  39.9 us (1%)
    reduce_scatter x1, waiting for transfers between devices, local(): lax.psum_scatter(ordered, 'dp', scatter_dimension=0, tiled=True)  1140 us
    ppermute x15, waiting for transfers between devices, local(): lax.ppermute(samples[at - 1], axis_name='dp', perm=[(t, (t - 1) % devs) f...  714 us
    dot_general x18, matrix products, matmul(): return jnp.dot(left, right, preferred_element_type=jnp.float32)  196 us
    unnamed x254, local copies, waits for them, and re-layouts  163 us
    ppermute x15, starting transfers between devices, local(): lax.ppermute(samples[at - 1], axis_name='dp', perm=[(t, (t - 1) % devs) f...  92.4 us
    reshape x6, local copies, waits for them, and re-layouts, assemble(): return pieces.reshape(row_blocks, col_blocks, block_size, block_size).tra...  67.7 us
  transfers between devices with their start and end apart: 19, of which 16 were waited for; matrix products, arithmetic and copies ran while one was open for 7% of the time, Pallas kernels for 0%

profile of v1, /device:TPU:0, one launch (start us, length us, event | category | flops | bytes accessed | tf_op | source)
XLA Modules:
  0.0 3138.7 jit_solution(18233350251541979582)
XLA Ops:
  14.2 55.6 %collective-permute-done = bf16[12,280,280]{2,1,0:T(8,128)(2,1)S(1)} collective-permute-done((bf16[12,280,280]{2,1,0:T(8,128)(2,1)}, bf16[12,280,280]{2,1,0:T(8,128)(2,1)S(1)}, u32[]{:S(2)}, u32[]{:S(2)}) %collective-permute-start) | collective-permute-done | bytes 1881632 | tf_op jit(solution)/shard_map/ppermute | solution.py:76
  77.2 54.4 %collective-permute-done.1 = bf16[12,280,280]{2,1,0:T(8,128)(2,1)S(1)} collective-permute-done((bf16[12,280,280]{2,1,0:T(8,128)(2,1)S(1)}, bf16[12,280,280]{2,1,0:T(8,128)(2,1)S(1)}, u32[]{:S(2)}, u32[]{:S(2)}) %collective-permute-start.1) | collective-permute-done | bytes 1881632 | tf_op jit(solution)/shard_map/ppermute | solution.py:76
  139.2 53.5 %collective-permute-done.2 = bf16[12,280,280]{2,1,0:T(8,128)(2,1)S(1)} collective-permute-done((bf16[12,280,280]{2,1,0:T(8,128)(2,1)S(1)}, bf16[12,280,280]{2,1,0:T(8,128)(2,1)S(1)}, u32[]{:S(2)}, u32[]{:S(2)}) %collective-permute-start.2) | collective-permute-done | bytes 1881632 | tf_op jit(solution)/shard_map/ppermute | solution.py:76
  200.2 52.5 %collective-permute-done.3 = bf16[12,280,280]{2,1,0:T(8,128)(2,1)S(1)} collective-permute-done((bf16[12,280,280]{2,1,0:T(8,128)(2,1)S(1)}, bf16[12,280,280]{2,1,0:T(8,128)(2,1)S(1)}, u32[]{:S(2)}, u32[]{:S(2)}) %collective-permute-start.3) | collective-permute-done | bytes 1881632 | tf_op jit(solution)/shard_map/ppermute | solution.py:76
  260.3 51.6 %collective-permute-done.4 = bf16[12,280,280]{2,1,0:T(8,128)(2,1)S(1)} collective-permute-done((bf16[12,280,280]{2,1,0:T(8,128)(2,1)S(1)}, bf16[12,280,280]{2,1,0:T(8,128)(2,1)S(1)}, u32[]{:S(2)}, u32[]{:S(2)}) %collective-permute-start.4) | collective-permute-done | bytes 1881632 | tf_op jit(solution)/shard_map/ppermute | solution.py:76
  319.4 50.7 %collective-permute-done.5 = bf16[12,280,280]{2,1,0:T(8,128)(2,1)S(1)} collective-permute-done((bf16[12,280,280]{2,1,0:T(8,128)(2,1)S(1)}, bf16[12,280,280]{2,1,0:T(8,128)(2,1)S(1)}, u32[]{:S(2)}, u32[]{:S(2)}) %collective-permute-start.5) | collective-permute-done | bytes 1881632 | tf_op jit(solution)/shard_map/ppermute | solution.py:76
  377.7 49.8 %collective-permute-done.6 = bf16[12,280,280]{2,1,0:T(8,128)(2,1)S(1)} collective-permute-done((bf16[12,280,280]{2,1,0:T(8,128)(2,1)S(1)}, bf16[12,280,280]{2,1,0:T(8,128)(2,1)S(1)}, u32[]{:S(2)}, u32[]{:S(2)}) %collective-permute-start.6) | collective-permute-done | bytes 1881632 | tf_op jit(solution)/shard_map/ppermute | solution.py:76
  435.0 48.8 %collective-permute-done.7 = bf16[12,280,280]{2,1,0:T(8,128)(2,1)S(1)} collective-permute-done((bf16[12,280,280]{2,1,0:T(8,128)(2,1)S(1)}, bf16[12,280,280]{2,1,0:T(8,128)(2,1)S(1)}, u32[]{:S(2)}, u32[]{:S(2)}) %collective-permute-start.7) | collective-permute-done | bytes 1881632 | tf_op jit(solution)/shard_map/ppermute | solution.py:76
  491.5 48.6 %collective-permute-done.8 = bf16[12,280,280]{2,1,0:T(8,128)(2,1)S(1)} collective-permute-done((bf16[12,280,280]{2,1,0:T(8,128)(2,1)S(1)}, bf16[12,280,280]{2,1,0:T(8,128)(2,1)S(1)}, u32[]{:S(2)}, u32[]{:S(2)}) %collective-permute-start.8) | collective-permute-done | bytes 1881632 | tf_op jit(solution)/shard_map/ppermute | solution.py:76
  547.6 48.6 %collective-permute-done.9 = bf16[12,280,280]{2,1,0:T(8,128)(2,1)S(1)} collective-permute-done((bf16[12,280,280]{2,1,0:T(8,128)(2,1)S(1)}, bf16[12,280,280]{2,1,0:T(8,128)(2,1)S(1)}, u32[]{:S(2)}, u32[]{:S(2)}) %collective-permute-start.9) | collective-permute-done | bytes 1881632 | tf_op jit(solution)/shard_map/ppermute | solution.py:76
  603.8 49.8 %collective-permute-done.10 = bf16[12,280,280]{2,1,0:T(8,128)(2,1)} collective-permute-done((bf16[12,280,280]{2,1,0:T(8,128)(2,1)S(1)}, bf16[12,280,280]{2,1,0:T(8,128)(2,1)}, u32[]{:S(2)}, u32[]{:S(2)}) %collective-permute-start.10) | collective-permute-done | bytes 1881632 | tf_op jit(solution)/shard_map/ppermute | solution.py:76
  660.4 49.4 %collective-permute-done.11 = bf16[12,280,280]{2,1,0:T(8,128)(2,1)} collective-permute-done((bf16[12,280,280]{2,1,0:T(8,128)(2,1)}, bf16[12,280,280]{2,1,0:T(8,128)(2,1)}, u32[]{:S(2)}, u32[]{:S(2)}) %collective-permute-start.11) | collective-permute-done | bytes 1881632 | tf_op jit(solution)/shard_map/ppermute | solution.py:76
  721.8 44.1 %collective-permute-done.12 = bf16[12,280,280]{2,1,0:T(8,128)(2,1)} collective-permute-done((bf16[12,280,280]{2,1,0:T(8,128)(2,1)}, bf16[12,280,280]{2,1,0:T(8,128)(2,1)}, u32[]{:S(2)}, u32[]{:S(2)}) %collective-permute-start.12) | collective-permute-done | bytes 1881632 | tf_op jit(solution)/shard_map/ppermute | solution.py:76
  783.6 38.3 %collective-permute-done.13 = bf16[12,280,280]{2,1,0:T(8,128)(2,1)S(1)} collective-permute-done((bf16[12,280,280]{2,1,0:T(8,128)(2,1)}, bf16[12,280,280]{2,1,0:T(8,128)(2,1)S(1)}, u32[]{:S(2)}, u32[]{:S(2)}) %collective-permute-start.13) | collective-permute-done | bytes 1881632 | tf_op jit(solution)/shard_map/ppermute | solution.py:76
  906.0 28.2 constant_dynamic-slice_fusion
  934.3 28.1 gather_fusion
  962.4 28.2 broadcast_select_fusion.1
  1264.6 30.9 fusion.8
  1485.2 28.5 reshape.801
  1672.3 56.0 %broadcast_multiply_fusion = f32[192,280,280]{2,1,0:T(8,128)} fusion(f32[192,280,280]{2,1,0:T(8,128)} %constant_dynamic-update-slice_fusion.32), kind=kLoop, calls=%fused_computation.4 | loop fusion | flops 15052800 | bytes 120422400 | tf_op jit(solution)/shard_map/mul | solution.py:260
  1728.3 56.3 %gather_fusion.1 = f32[192,280,280]{2,1,0:T(8,128)} fusion(f32[192,280,280]{2,1,0:T(8,128)} %broadcast_multiply_fusion, s32[1024]{0:T(1024)} %pad_clamp_fusion), kind=kCustom, calls=%fused_computation.1 | custom fusion | bytes 120423168 | tf_op jit(solution)/shard_map/jit(_take)/gather | solution.py:269
  1784.5 54.2 %broadcast_select_fusion = f32[192,280,280]{2,1,0:T(8,128)} fusion(f32[192,280,280]{2,1,0:T(8,128)} %gather_fusion.1, pred[192]{0:T(512)(128)(4,1)S(1)} %copy-done.79), kind=kLoop, calls=%fused_computation.3 | loop fusion | flops 15052800 | bytes 120422592 | tf_op jit(solution)/shard_map/jit(_take)/select_n | solution.py:269
  1838.8 1137.9 %reduce-scatter.2.cloned.1.call-done = f32[12,280,280]{2,1,0:T(8,128)} async-done(((f32[192,280,280]{2,1,0:T(8,128)}), f32[12,280,280]{2,1,0:T(8,128)}) %reduce-scatter.2.cloned.1.call-update) | async-done | bytes 3763216 | tf_op jit(solution)/shard_map/reduce_scatter | solution.py:270
  3009.4 39.9 %psum.46 = f32[4,1120]{1,0:T(4,128)S(1)} all-reduce(f32[4,1120]{1,0:T(4,128)S(1)} %maximum_multiply_fusion.1), channel_id=1, replica_groups=mesh['dp'=16,'seq'=2] {'dp','seq'}, use_global_device_ids=true, to_apply=%region_20.21 | all-reduce | flops 4480 | bytes 35840 | tf_op jit(solution)/shard_map/psum | solution.py:256
  (401 shorter events, 938.5 us)
Async XLA Ops:
  7.2 768.3 %copy-start.5 = (bf16[1,1024,1120]{1,2,0:T(8,128)(2,1)S(1)}, bf16[1,1024,1120]{1,2,0:T(8,128)(2,1)}, u32[]{:S(2)}) copy-start(bf16[1,1024,1120]{1,2,0:T(8,128)(2,1)} %param.18) | copy-start | bytes 6881284
  7.2 1181.8 %all-reduce.10.cloned.1.call-start = ((), (), s32[]{:S(2)}) async-start(), calls=%async_computation.4 | async-start | bytes 1146880 | tf_op jit(solution)/shard_map/psum | solution.py:15
  7.2 62.5 %collective-permute-start = (bf16[12,280,280]{2,1,0:T(8,128)(2,1)}, bf16[12,280,280]{2,1,0:T(8,128)(2,1)S(1)}, u32[]{:S(2)}, u32[]{:S(2)}) collective-permute-start(bf16[12,280,280]{2,1,0:T(8,128)(2,1)} %param.25), channel_id=1, source_target_pairs={{0,30},{2,0},{4,2},{6,4},{8,6},{10,8},{12,10},{14,12},{16,14},{18,... | collective-permute-start | bytes 5644808 | tf_op jit(solution)/shard_map/ppermute | solution.py:76
  71.3 60.3 %collective-permute-start.1 = (bf16[12,280,280]{2,1,0:T(8,128)(2,1)S(1)}, bf16[12,280,280]{2,1,0:T(8,128)(2,1)S(1)}, u32[]{:S(2)}, u32[]{:S(2)}) collective-permute-start(bf16[12,280,280]{2,1,0:T(8,128)(2,1)S(1)} %collective-permute-done), channel_id=1, source_target_pairs={{0,30},{2,0},{4,2},{6,4},{8,6},{10,8},{12,10},{14,12},{16,14},{18,... | collective-permute-start | bytes 5644808 | tf_op jit(solution)/shard_map/ppermute | solution.py:76
  133.1 59.5 %collective-permute-start.2 = (bf16[12,280,280]{2,1,0:T(8,128)(2,1)S(1)}, bf16[12,280,280]{2,1,0:T(8,128)(2,1)S(1)}, u32[]{:S(2)}, u32[]{:S(2)}) collective-permute-start(bf16[12,280,280]{2,1,0:T(8,128)(2,1)S(1)} %collective-permute-done.1), channel_id=1, source_target_pairs={{0,30},{2,0},{4,2},{6,4},{8,6},{10,8},{12,10},{14,12},{16,14},{18,... | collective-permute-start | bytes 5644808 | tf_op jit(solution)/shard_map/ppermute | solution.py:76
  194.1 58.6 %collective-permute-start.3 = (bf16[12,280,280]{2,1,0:T(8,128)(2,1)S(1)}, bf16[12,280,280]{2,1,0:T(8,128)(2,1)S(1)}, u32[]{:S(2)}, u32[]{:S(2)}) collective-permute-start(bf16[12,280,280]{2,1,0:T(8,128)(2,1)S(1)} %collective-permute-done.2), channel_id=1, source_target_pairs={{0,30},{2,0},{4,2},{6,4},{8,6},{10,8},{12,10},{14,12},{16,14},{18,... | collective-permute-start | bytes 5644808 | tf_op jit(solution)/shard_map/ppermute | solution.py:76
  254.2 57.7 %collective-permute-start.4 = (bf16[12,280,280]{2,1,0:T(8,128)(2,1)S(1)}, bf16[12,280,280]{2,1,0:T(8,128)(2,1)S(1)}, u32[]{:S(2)}, u32[]{:S(2)}) collective-permute-start(bf16[12,280,280]{2,1,0:T(8,128)(2,1)S(1)} %collective-permute-done.3), channel_id=1, source_target_pairs={{0,30},{2,0},{4,2},{6,4},{8,6},{10,8},{12,10},{14,12},{16,14},{18,... | collective-permute-start | bytes 5644808 | tf_op jit(solution)/shard_map/ppermute | solution.py:76
  313.3 56.8 %collective-permute-start.5 = (bf16[12,280,280]{2,1,0:T(8,128)(2,1)S(1)}, bf16[12,280,280]{2,1,0:T(8,128)(2,1)S(1)}, u32[]{:S(2)}, u32[]{:S(2)}) collective-permute-start(bf16[12,280,280]{2,1,0:T(8,128)(2,1)S(1)} %collective-permute-done.4), channel_id=1, source_target_pairs={{0,30},{2,0},{4,2},{6,4},{8,6},{10,8},{12,10},{14,12},{16,14},{18,... | collective-permute-start | bytes 5644808 | tf_op jit(solution)/shard_map/ppermute | solution.py:76
  371.6 55.8 %collective-permute-start.6 = (bf16[12,280,280]{2,1,0:T(8,128)(2,1)S(1)}, bf16[12,280,280]{2,1,0:T(8,128)(2,1)S(1)}, u32[]{:S(2)}, u32[]{:S(2)}) collective-permute-start(bf16[12,280,280]{2,1,0:T(8,128)(2,1)S(1)} %collective-permute-done.5), channel_id=1, source_target_pairs={{0,30},{2,0},{4,2},{6,4},{8,6},{10,8},{12,10},{14,12},{16,14},{18,... | collective-permute-start | bytes 5644808 | tf_op jit(solution)/shard_map/ppermute | solution.py:76
  428.9 54.9 %collective-permute-start.7 = (bf16[12,280,280]{2,1,0:T(8,128)(2,1)S(1)}, bf16[12,280,280]{2,1,0:T(8,128)(2,1)S(1)}, u32[]{:S(2)}, u32[]{:S(2)}) collective-permute-start(bf16[12,280,280]{2,1,0:T(8,128)(2,1)S(1)} %collective-permute-done.6), channel_id=1, source_target_pairs={{0,30},{2,0},{4,2},{6,4},{8,6},{10,8},{12,10},{14,12},{16,14},{18,... | collective-permute-start | bytes 5644808 | tf_op jit(solution)/shard_map/ppermute | solution.py:76
  485.4 54.6 %collective-permute-start.8 = (bf16[12,280,280]{2,1,0:T(8,128)(2,1)S(1)}, bf16[12,280,280]{2,1,0:T(8,128)(2,1)S(1)}, u32[]{:S(2)}, u32[]{:S(2)}) collective-permute-start(bf16[12,280,280]{2,1,0:T(8,128)(2,1)S(1)} %collective-permute-done.7), channel_id=1, source_target_pairs={{0,30},{2,0},{4,2},{6,4},{8,6},{10,8},{12,10},{14,12},{16,14},{18,... | collective-permute-start | bytes 5644808 | tf_op jit(solution)/shard_map/ppermute | solution.py:76
  541.5 54.7 %collective-permute-start.9 = (bf16[12,280,280]{2,1,0:T(8,128)(2,1)S(1)}, bf16[12,280,280]{2,1,0:T(8,128)(2,1)S(1)}, u32[]{:S(2)}, u32[]{:S(2)}) collective-permute-start(bf16[12,280,280]{2,1,0:T(8,128)(2,1)S(1)} %collective-permute-done.8), channel_id=1, source_target_pairs={{0,30},{2,0},{4,2},{6,4},{8,6},{10,8},{12,10},{14,12},{16,14},{18,... | collective-permute-start | bytes 5644808 | tf_op jit(solution)/shard_map/ppermute | solution.py:76
  597.7 55.8 %collective-permute-start.10 = (bf16[12,280,280]{2,1,0:T(8,128)(2,1)S(1)}, bf16[12,280,280]{2,1,0:T(8,128)(2,1)}, u32[]{:S(2)}, u32[]{:S(2)}) collective-permute-start(bf16[12,280,280]{2,1,0:T(8,128)(2,1)S(1)} %collective-permute-done.9), channel_id=1, source_target_pairs={{0,30},{2,0},{4,2},{6,4},{8,6},{10,8},{12,10},{14,12},{16,14},{18,... | collective-permute-start | bytes 5644808 | tf_op jit(solution)/shard_map/ppermute | solution.py:76
  653.5 56.3 %collective-permute-start.11 = (bf16[12,280,280]{2,1,0:T(8,128)(2,1)}, bf16[12,280,280]{2,1,0:T(8,128)(2,1)}, u32[]{:S(2)}, u32[]{:S(2)}) collective-permute-start(bf16[12,280,280]{2,1,0:T(8,128)(2,1)} %collective-permute-done.10), channel_id=1, source_target_pairs={{0,30},{2,0},{4,2},{6,4},{8,6},{10,8},{12,10},{14,12},{16,14},{18,... | collective-permute-start | bytes 5644808 | tf_op jit(solution)/shard_map/ppermute | solution.py:76
  709.8 56.2 %collective-permute-start.12 = (bf16[12,280,280]{2,1,0:T(8,128)(2,1)}, bf16[12,280,280]{2,1,0:T(8,128)(2,1)}, u32[]{:S(2)}, u32[]{:S(2)}) collective-permute-start(bf16[12,280,280]{2,1,0:T(8,128)(2,1)} %collective-permute-done.11), channel_id=1, source_target_pairs={{0,30},{2,0},{4,2},{6,4},{8,6},{10,8},{12,10},{14,12},{16,14},{18,... | collective-permute-start | bytes 5644808 | tf_op jit(solution)/shard_map/ppermute | solution.py:76
  765.9 56.0 %collective-permute-start.13 = (bf16[12,280,280]{2,1,0:T(8,128)(2,1)}, bf16[12,280,280]{2,1,0:T(8,128)(2,1)S(1)}, u32[]{:S(2)}, u32[]{:S(2)}) collective-permute-start(bf16[12,280,280]{2,1,0:T(8,128)(2,1)} %collective-permute-done.12), channel_id=1, source_target_pairs={{0,30},{2,0},{4,2},{6,4},{8,6},{10,8},{12,10},{14,12},{16,14},{18,... | collective-permute-start | bytes 5644808 | tf_op jit(solution)/shard_map/ppermute | solution.py:76
  775.9 290.5 %copy-start.56 = (f32[1024]{0:T(1024)}, f32[1024]{0:T(1024)S(1)}, u32[]{:S(2)}) copy-start(f32[1024]{0:T(1024)S(1)} %broadcast_multiply_fusion.4) | copy-start | bytes 12292
  777.1 289.2 %copy-start.62 = (f32[1024]{0:T(1024)}, f32[1024]{0:T(1024)S(1)}, u32[]{:S(2)}) copy-start(f32[1024]{0:T(1024)S(1)} %fusion.95) | copy-start | bytes 12292
  778.4 288.0 %copy-start.54 = (f32[1120]{0:T(1024)}, f32[1120]{0:T(1024)S(1)}, u32[]{:S(2)}) copy-start(f32[1120]{0:T(1024)S(1)} %get-tuple-element.94) | copy-start | bytes 13444
  778.4 288.0 %copy-start.64 = (f32[1120]{0:T(1024)}, f32[1120]{0:T(1024)S(1)}, u32[]{:S(2)}) copy-start(f32[1120]{0:T(1024)S(1)} %get-tuple-element.63) | copy-start | bytes 13444
  822.0 49.2 %collective-permute-start.14 = (bf16[12,280,280]{2,1,0:T(8,128)(2,1)S(1)}, bf16[12,280,280]{2,1,0:T(8,128)(2,1)S(1)}, u32[]{:S(2)}, u32[]{:S(2)}) collective-permute-start(bf16[12,280,280]{2,1,0:T(8,128)(2,1)S(1)} %collective-permute-done.13), channel_id=1, source_target_pairs={{0,30},{2,0},{4,2},{6,4},{8,6},{10,8},{12,10},{14,12},{16,14},{18,... | collective-permute-start | bytes 5644808 | tf_op jit(solution)/shard_map/ppermute | solution.py:76
  1066.3 517.6 %all-reduce.8.cloned.1.call-start = ((), (), s32[]{:S(2)}) async-start(), calls=%async_computation.3 | async-start | bytes 2293760 | tf_op jit(solution)/shard_map/psum | solution.py:227
  1553.4 1423.4 %reduce-scatter.2.cloned.1.call-start = ((), (), s32[]{:S(2)}) async-start(), calls=%async_computation.1 | async-start | bytes 87736320 | tf_op jit(solution)/shard_map/reduce_scatter | solution.py:270
  1838.7 1212.5 %all-reduce.6.cloned.1.call-start = ((), (), s32[]{:S(2)}) async-start(), calls=%async_computation.2 | async-start | bytes 10321920 | tf_op jit(solution)/shard_map/psum | solution.py:271
  (99 other events, 1585.6 us)
Sparse Core Ops, SparseCore 0:
  1066.4 20.7 all-reduce.9
  1553.5 21.6 all-reduce.7
  1838.9 1137.8 reduce-scatter.1
  2979.3 28.9 all-reduce.5
